TPU v7x, 256 devices: a whole 4x4x8 slice. The times are simulated.
256 devices in a mesh: leaf: 8 (over y, core), front: 32 (over x, z).
Axes of the slice: x: 4, y: 4, z: 8, core: 2. Of those that a mesh axis runs over, the one named last changes fastest.
Arguments:
- child_fronts: float32 [8, 4096, 1, 32, 128], P('leaf', None, None, 'front'), as said below
- parent_front: float32 [8, 8, 128, 2, 32, 128], P(None, 'leaf', None, None, 'front'), as said below
- child_map: int32 [8, 24], replicated, may hold values from 0 to 63, as said below
Outputs:
- child_result: float32 [8, 4096, 1, 32, 128], P('leaf', None, None, 'front')
- parent_result: float32 [8, 8, 128, 2, 32, 128], P(None, 'leaf', None, None, 'front')
Inputs may be any that keep to these rules, and one draw needn't show every extreme that they name: Row g gives, for each update block v of child g, the parent block that receives it. The entries of a row are distinct, child_map[g, v] mod 32 equals (8 + v) mod 32, and every child's last update block goes to the parent's last block. `child_fronts`: each front is symmetric positive definite. `parent_front`: the parent front is symmetric positive definite.
All inputs are finite; a program needn't handle non-finite values.
Results may differ from a plain program's by a relative error of at most 0.000059.
Values sent between devices are 32-bit elements; how exact they have to be, the bound alone decides.
No kernel may reach another device: no remote copies, remote signals or barrier semaphores. Data moves between devices by JAX's collectives and lax.ppermute only.
A program may use at most 256 MiB of HBM per device.

v0:
```python
import jax
import jax.numpy as jnp
from jax import lax
from jax.sharding import PartitionSpec as P

CHILD_PIVOTS = 8
PARENT_PIVOTS = 2


def from_root(value, axis, source):
    kept = jnp.where(lax.axis_index(axis) == source, value, 0).astype(value.dtype)
    return lax.psum(kept, axis)


def solve_rows(factor, rows):
    return jax.scipy.linalg.solve_triangular(factor, rows.T, lower=True).T


def body(child_fronts, parent_front, child_map):
    front_count = lax.axis_size("front")
    leaf_count = lax.axis_size("leaf")
    front_pos = lax.axis_index("front")
    leaf_pos = lax.axis_index("leaf")
    block = child_fronts.shape[4]
    child_order = child_fronts.shape[1]
    child_slots = child_fronts.shape[2]
    blocks_total = child_order // block
    pivots = CHILD_PIVOTS
    highest = lax.Precision.HIGHEST
    matrix = child_fronts.reshape(child_order, child_slots * block)
    column_ids = jnp.arange(child_slots * block) // block * front_count + front_pos
    slot_ids = jnp.arange(child_slots) * front_count + front_pos
    panel_slots = (pivots + front_count - 1) // front_count
    piece_rows = child_order // front_count
    width = pivots * block
    leading = matrix.reshape(front_count, piece_rows, panel_slots, 1, block)
    spread = lax.all_to_all(leading, "front", split_axis=0, concat_axis=3, tiled=True)
    rows_part = spread.reshape(piece_rows, panel_slots * front_count * block)[:, :width]
    panel = lax.all_gather(rows_part, "front", axis=0, tiled=True)
    factored = []
    for pivot in range(pivots):
        start = pivot * block
        finish = start + block
        current = panel[:, start:finish]
        if factored:
            done = jnp.concatenate(factored, 1)
            current = current - jnp.dot(done, done[start:finish].T, precision=highest)
        factor = jnp.linalg.cholesky(current[start:finish])
        below = solve_rows(factor, current[finish:])
        factored.append(jnp.concatenate([jnp.zeros((start, block), jnp.float32), factor, below], 0))
    panel = jnp.concatenate(factored, 1)
    lower_rows = panel[width:]
    padded = jnp.concatenate([jnp.zeros((width, width), jnp.float32), lower_rows], 0)
    picked = jnp.take(padded.reshape(blocks_total, block, width), slot_ids, axis=0)
    picked = picked.reshape(child_slots * block, width)
    update = jnp.dot(lower_rows, picked.T, precision=highest)
    matrix = jnp.concatenate([matrix[:width], matrix[width:] - update], 0)
    pivot_columns = jnp.take(
        panel.reshape(child_order, pivots, block), jnp.clip(slot_ids, 0, pivots - 1), axis=1
    )
    pivot_columns = pivot_columns.reshape(child_order, child_slots * block)
    matrix = jnp.where((column_ids < pivots)[None, :], pivot_columns, matrix)
    row_blocks = jnp.arange(child_order) // block
    matrix = jnp.where(
        (row_blocks[:, None] < pivots) & (column_ids[None, :] >= pivots), 0.0, matrix
    )
    child_result = matrix.reshape(child_fronts.shape)
    first_slot = pivots // front_count
    update_count = blocks_total - pivots
    quota = update_count // leaf_count
    kept_slots = child_slots - first_slot
    outgoing = matrix[pivots * block :, first_slot * block :].reshape(
        quota, leaf_count, block, kept_slots, block
    )
    received = lax.all_to_all(outgoing, "leaf", split_axis=1, concat_axis=1, tiled=True)
    parent_rslots = parent_front.shape[0]
    parent_cslots = parent_front.shape[3]
    groups = child_map.shape[0]
    row_map = lax.dynamic_index_in_dim(
        child_map.reshape(groups, quota, leaf_count), leaf_pos, axis=2, keepdims=False
    )
    row_onehot = (
        (row_map // leaf_count)[:, :, None] == jnp.arange(parent_rslots)[None, None, :]
    ).astype(jnp.float32)
    col_blocks = jnp.arange(first_slot, child_slots) * front_count + front_pos - pivots
    valid = col_blocks >= 0
    col_map = jnp.take(child_map, jnp.clip(col_blocks, 0, update_count - 1), axis=1)
    col_match = (col_map // front_count)[:, :, None] == jnp.arange(parent_cslots)[None, None, :]
    col_onehot = (valid[None, :, None] & col_match).astype(jnp.float32)
    placed = jnp.einsum("gqa,qgxcy->gaxcy", row_onehot, received, precision=highest)
    summed = jnp.einsum("gcb,gaxcy->axby", col_onehot, placed, precision=highest)
    parent = parent_front.reshape(parent_rslots * block, parent_cslots * block)
    parent = parent + summed.reshape(parent_rslots * block, parent_cslots * block)
    prow_ids = jnp.arange(parent_rslots * block) // block * leaf_count + leaf_pos
    pcol_ids = jnp.arange(parent_cslots * block) // block * front_count + front_pos
    col_slot_ids = jnp.arange(parent_cslots) * front_count + front_pos
    parent_blocks = parent_rslots * leaf_count
    for pivot in range(PARENT_PIVOTS):
        col_root = pivot % front_count
        col_slot = pivot // front_count
        column = from_root(parent[:, col_slot * block : (col_slot + 1) * block], "front", col_root)
        whole = lax.all_gather(
            column.reshape(parent_rslots, 1, block, block), "leaf", axis=1, tiled=True
        )
        whole = whole.reshape(parent_blocks * block, block)
        factor = jnp.linalg.cholesky(whole[pivot * block : (pivot + 1) * block])
        above = jnp.arange(parent_blocks * block) // block <= pivot
        panel_all = jnp.where(above[:, None], 0.0, solve_rows(factor, whole))
        panel_local = lax.dynamic_index_in_dim(
            panel_all.reshape(parent_rslots, leaf_count, block, block),
            leaf_pos,
            axis=1,
            keepdims=False,
        )
        panel_local = panel_local.reshape(parent_rslots * block, block)
        panel_cols = jnp.take(panel_all.reshape(parent_blocks, block, block), col_slot_ids, axis=0)
        panel_cols = panel_cols.reshape(parent_cslots * block, block)
        parent = parent - jnp.dot(panel_local, panel_cols.T, precision=highest)
        new_column = jnp.where(
            (prow_ids == pivot)[:, None], jnp.tile(factor, (parent_rslots, 1)), panel_local
        )
        parent = jnp.where(
            (pcol_ids == pivot)[None, :], jnp.tile(new_column, (1, parent_cslots)), parent
        )
    parent = jnp.where(
        (prow_ids[:, None] < PARENT_PIVOTS) & (pcol_ids[None, :] >= PARENT_PIVOTS), 0.0, parent
    )
    parent_result = parent.reshape(parent_front.shape)
    return (child_result, parent_result)


def solution(mesh):
    return jax.shard_map(
        body,
        mesh=mesh,
        in_specs=(
            P("leaf", None, None, "front", None),
            P(None, "leaf", None, None, "front", None),
            P(),
        ),
        out_specs=(
            P("leaf", None, None, "front", None),
            P(None, "leaf", None, None, "front", None),
        ),
        check_vma=False,
    )
```

profile of v0, /device:TPU:1, one launch (start us, length us, event | category | flops | bytes accessed | tf_op | source)
XLA Modules:
  0.0 1122.5 jit_solution(9140086913253102955)
XLA Ops:
  9.1 58.8 %all_to_all.20 = f32[32,128,1,1,128]{1,4,3,2,0:T(8,128)S(1)} all-to-all(f32[32,128,1,1,128]{1,4,3,2,0:T(8,128)S(1)} %copy.144), channel_id=1, replica_groups=mesh['leaf'=8,'front'=32] {'front'}, dimensions={0} | all-to-all | bytes 4194304 | tf_op jit(solution)/shard_map/all_to_all | solution.py:37
  70.8 147.3 %all-gather.4.cloned.1.call-done = f32[4096,1024]{0,1:T(8,128)} async-done(((f32[128,1024]{0,1:T(8,128)}), f32[4096,1024]{0,1:T(8,128)}) %all-gather.4.cloned.1.call-update) | async-done | bytes 16777232 | tf_op jit(solution)/shard_map/all_gather | solution.py:39
  219.9 11.7 %cholesky.164 = f32[128,128]{1,0:T(8,128)S(1)} custom-call(f32[128,128]{1,0:T(8,128)S(1)} %fusion.173), custom_call_target="Cholesky" | custom-call | tf_op jit(solution)/shard_map/jit(cholesky)/cholesky | solution.py:48
  233.0 9.8 custom-call.37
  256.6 11.9 %cholesky.175 = f32[128,128]{1,0:T(8,128)S(1)} custom-call(f32[128,128]{1,0:T(8,128)S(1)} %fusion.171), custom_call_target="Cholesky" | custom-call | tf_op jit(solution)/shard_map/jit(cholesky)/cholesky | solution.py:48
  291.5 12.1 %cholesky.186 = f32[128,128]{1,0:T(8,128)S(1)} custom-call(f32[128,128]{1,0:T(8,128)S(1)} %fusion.169), custom_call_target="Cholesky" | custom-call | tf_op jit(solution)/shard_map/jit(cholesky)/cholesky | solution.py:48
  329.4 11.7 %cholesky.197 = f32[128,128]{1,0:T(8,128)S(1)} custom-call(f32[128,128]{1,0:T(8,128)S(1)} %fusion.167), custom_call_target="Cholesky" | custom-call | tf_op jit(solution)/shard_map/jit(cholesky)/cholesky | solution.py:48
  357.0 10.2 fusion.41
  369.6 11.7 %cholesky.208 = f32[128,128]{1,0:T(8,128)S(1)} custom-call(f32[128,128]{1,0:T(8,128)S(1)} %fusion.165), custom_call_target="Cholesky" | custom-call | tf_op jit(solution)/shard_map/jit(cholesky)/cholesky | solution.py:48
  414.2 10.0 convolution_subtract_fusion.1
  424.3 11.7 %cholesky.219 = f32[128,128]{1,0:T(8,128)S(1)} custom-call(f32[128,128]{1,0:T(8,128)S(1)} %fusion.163), custom_call_target="Cholesky" | custom-call | tf_op jit(solution)/shard_map/jit(cholesky)/cholesky | solution.py:48
  454.9 10.7 convolution_subtract_fusion
  465.7 11.7 %cholesky.230 = f32[128,128]{1,0:T(8,128)S(1)} custom-call(f32[128,128]{1,0:T(8,128)S(1)} %fusion.161), custom_call_target="Cholesky" | custom-call | tf_op jit(solution)/shard_map/jit(cholesky)/cholesky | solution.py:48
  495.4 12.9 %convolution_subtract_fusion.4 = f32[4096,128]{0,1:T(8,128)S(1)} fusion(f32[4096,896]{0,1:T(8,128)} %get-tuple-element.91, f32[4096,1024]{0,1:T(8,128)} %all-gather.4.cloned.1.call-done), kind=kOutput, calls=%fused_computation.48 | convolution fusion | flops 5637668864 | bytes 19333120 | tf_op jit(solution)/shard_map/dot_general | solution.py:47
  508.4 11.7 %cholesky.241 = f32[128,128]{1,0:T(8,128)S(1)} custom-call(f32[128,128]{1,0:T(8,128)S(1)} %fusion.159), custom_call_target="Cholesky" | custom-call | tf_op jit(solution)/shard_map/jit(cholesky)/cholesky | solution.py:48
  537.0 10.8 slice.282
  566.9 21.1 %convolution_subtract_fusion.5 = f32[3072,128]{1,0:T(8,128)} fusion(f32[128,1024]{0,1:T(8,128)S(1)} %bitcast.252, f32[1,4096,1,1,128]{4,1,3,2,0:T(8,128)S(1)} %bitcast.235, f32[4096,1024]{0,1:T(8,128)S(1)} %bitcast.221), kind=kOutput, calls=%fused_computation.66 | convolution fusion | flops 4832231424 | bytes 16252928 | tf_op jit(solution)/shard_map/dot_general | solution.py:56
  604.2 19.8 %all-to-all-done.1 = f32[3,8,128,1,128]{4,2,0,3,1:T(8,128)} async-done(((f32[3,8,128,1,128]{4,2,0,3,1:T(8,128)}), f32[3,8,128,1,128]{4,2,0,3,1:T(8,128)}, u32[]{:S(2)}, u32[]{:S(2)}) %all-to-all-start.1) | async-done | bytes 1572896 | tf_op jit(solution)/shard_map/all_to_all | solution.py:75
  635.1 138.2 %all-reduce.4.cloned.1.call-done = f32[8,1,128,128]{3,2,0,1:T(8,128)} async-done(((f32[8,1,128,128]{3,2,0,1:T(8,128)}), f32[8,1,128,128]{3,2,0,1:T(8,128)}) %all-reduce.4.cloned.1.call-update) | async-done | bytes 524304 | tf_op jit(solution)/shard_map/psum | solution.py:12
  773.6 38.3 %all-gather.6.cloned.1.call-done = f32[8,8,128,128]{3,2,0,1:T(8,128)} async-done(((f32[8,1,128,128]{3,2,0,1:T(8,128)}), f32[8,8,128,128]{3,2,0,1:T(8,128)}) %all-gather.6.cloned.1.call-update) | async-done | bytes 4194320 | tf_op jit(solution)/shard_map/all_gather | solution.py:102
  825.8 11.7 %cholesky.252 = f32[128,128]{1,0:T(8,128)S(1)} custom-call(f32[128,128]{1,0:T(8,128)S(1)} %fusion.157), custom_call_target="Cholesky" | custom-call | tf_op jit(solution)/shard_map/jit(cholesky)/cholesky | solution.py:106
  872.6 142.5 %all-reduce.6.cloned.1.call-done = f32[8,1,128,128]{3,2,0,1:T(8,128)} async-done(((f32[8,1,128,128]{3,2,0,1:T(8,128)}), f32[8,1,128,128]{3,2,0,1:T(8,128)}) %all-reduce.6.cloned.1.call-update) | async-done | bytes 524304 | tf_op jit(solution)/shard_map/psum | solution.py:12
  1020.6 33.0 %all-gather.8.cloned.1.call-done = f32[8,8,128,128]{3,2,0,1:T(8,128)} async-done(((f32[8,1,128,128]{3,2,0,1:T(8,128)}), f32[8,8,128,128]{3,2,0,1:T(8,128)}) %all-gather.8.cloned.1.call-update) | async-done | bytes 4194320 | tf_op jit(solution)/shard_map/all_gather | solution.py:102
  1067.3 11.7 %cholesky.263 = f32[128,128]{1,0:T(8,128)S(1)} custom-call(f32[128,128]{1,0:T(8,128)S(1)} %fusion.155), custom_call_target="Cholesky" | custom-call | tf_op jit(solution)/shard_map/jit(cholesky)/cholesky | solution.py:106
  (228 shorter events, 326.0 us)
Async XLA Ops:
  7.2 211.0 %all-gather.4.cloned.1.call-start = ((), (), s32[]{:S(2)}) async-start(), calls=%async_computation.2 | async-start | bytes 17301504 | tf_op jit(solution)/shard_map/all_gather | solution.py:39
  68.9 177.4 %copy-start.17 = (pred[4096]{0:T(1024)(128)(4,1)}, pred[4096]{0:T(1024)(128)(4,1)S(1)}, u32[]{:S(2)}) copy-start(pred[4096]{0:T(1024)(128)(4,1)S(1)} %fusion.195) | copy-start | bytes 12292
  368.6 28.3 %copy-start.2 = (f32[3840,128]{0,1:T(8,128)S(1)}, f32[3840,128]{0,1:T(8,128)}, u32[]{:S(2)}) copy-start(f32[3840,128]{0,1:T(8,128)} %fusion.62) | copy-start | bytes 5898244
  396.9 4.4 copy-start.7
  401.3 4.3 copy-start.8
  405.6 4.2 copy-start.9
  547.8 19.0 %slice-start = ((s8[16777216]{0:T(1024)(128)(4,1)}), s8[4194304]{0:T(1024)(128)(4,1)S(1)}, s32[]{:S(2)}) async-start(s8[16777216]{0:T(1024)(128)(4,1)} %bitcast.220), calls=%async_computation.7 | async-start | bytes 8388608
  547.8 19.0 %slice-start.1 = ((s8[16777216]{0:T(1024)(128)(4,1)}), s8[4194304]{0:T(1024)(128)(4,1)S(1)}, s32[]{:S(2)}) async-start(s8[16777216]{0:T(1024)(128)(4,1)} %bitcast.220), calls=%async_computation.8 | async-start | bytes 8388608
  555.2 11.6 %slice-start.2 = ((s8[16777216]{0:T(1024)(128)(4,1)}), s8[4194304]{0:T(1024)(128)(4,1)S(1)}, s32[]{:S(2)}) async-start(s8[16777216]{0:T(1024)(128)(4,1)} %bitcast.220), calls=%async_computation.9 | async-start | bytes 8388608
  555.2 11.6 %slice-start.3 = ((s8[16777216]{0:T(1024)(128)(4,1)}), s8[4194304]{0:T(1024)(128)(4,1)S(1)}, s32[]{:S(2)}) async-start(s8[16777216]{0:T(1024)(128)(4,1)} %bitcast.220), calls=%async_computation.10 | async-start | bytes 8388608
  555.2 11.6 %copy-start.4 = (f32[1,4096,1,1,128]{4,3,2,1,0:T(1,128)S(1)}, f32[1,4096,1,1,128]{4,3,2,1,0:T(1,128)}, u32[]{:S(2)}) copy-start(f32[1,4096,1,1,128]{4,3,2,1,0:T(1,128)} %param.8) | copy-start | bytes 6291460
  595.6 8.0 copy-start.19
  595.6 28.4 %all-to-all-start.1 = ((f32[3,8,128,1,128]{4,2,0,3,1:T(8,128)}), f32[3,8,128,1,128]{4,2,0,3,1:T(8,128)}, u32[]{:S(2)}, u32[]{:S(2)}) async-start(f32[3,8,128,1,128]{4,2,0,3,1:T(8,128)} %copy.181), calls=%async_computation.1 | async-start | bytes 3145728 | tf_op jit(solution)/shard_map/all_to_all | solution.py:75
  603.2 170.1 %all-reduce.4.cloned.1.call-start = ((), (), s32[]{:S(2)}) async-start(), calls=%async_computation.3 | async-start | bytes 1048576 | tf_op jit(solution)/shard_map/psum | solution.py:12
  628.8 4.3 copy-start.16
  635.1 176.9 %all-gather.6.cloned.1.call-start = ((), (), s32[]{:S(2)}) async-start(), calls=%async_computation.4 | async-start | bytes 4718592 | tf_op jit(solution)/shard_map/all_gather | solution.py:102
  773.3 241.9 %all-reduce.6.cloned.1.call-start = ((), (), s32[]{:S(2)}) async-start(), calls=%async_computation.5 | async-start | bytes 1048576 | tf_op jit(solution)/shard_map/psum | solution.py:12
  822.8 2.0 copy-start.12
  857.2 1.9 copy-start.1
  860.1 8.6 copy-start.11
  869.3 145.9 %copy-start.18 = (pred[4096]{0:T(1024)(128)(4,1)S(1)}, pred[4096]{0:T(1024)(128)(4,1)}, u32[]{:S(2)}) copy-start(pred[4096]{0:T(1024)(128)(4,1)} %copy-done.17) | copy-start | bytes 12292
  872.6 180.9 %all-gather.8.cloned.1.call-start = ((), (), s32[]{:S(2)}) async-start(), calls=%async_computation.6 | async-start | bytes 4718592 | tf_op jit(solution)/shard_map/all_gather | solution.py:102
  1064.4 1.9 copy-start.13
  1098.9 1.9 copy-start
  (7 other events, 9.1 us)
Sparse Core Ops, SparseCore 0:
  68.9 149.1 all-gather.3
  635.2 138.0 all-reduce.3
  775.3 36.6 all-gather.5
  872.7 142.3 all-reduce.5
  1016.9 36.6 all-gather.7
where the time goes:
time: 1130 us; the launch traced here: 1120 us
  waiting for transfers between devices  519 us (46%)
  other arithmetic  281 us (25%)
  matrix products  142 us (13%)
  local copies, waits for them, and re-layouts  98.3 us (9%)
  blocking collectives  58.8 us (5%)
  between operations  15.4 us (1%)
    psum x2, waiting for transfers between devices, from_root(): return lax.psum(kept, axis)  281 us
    all_gather x1, waiting for transfers between devices, body(): panel = lax.all_gather(rows_part, 'front', axis=0, tiled=True)  147 us
    another operation x20, other arithmetic, solve_rows(): return jax.scipy.linalg.solve_triangular(factor, rows.T, lower=True).T  105 us
    another operation x24, other arithmetic, body(): factor = jnp.linalg.cholesky(current[start:finish])  99.7 us
    all_gather x2, waiting for transfers between devices, body(): lax.all_gather(column.reshape(parent_rslots, 1, block, block), 'leaf', ax...  71.3 us
    dot_general x7, matrix products, body(): current = current - jnp.dot(done, done[start:finish].T, precision=highest)  59.9 us
    all_to_all x1, blocking collectives, body(): lax.all_to_all(leading, 'front', split_axis=0, concat_axis=3, tiled=True)  58.8 us
    another operation x10, matrix products, solve_rows(): return jax.scipy.linalg.solve_triangular(factor, rows.T, lower=True).T  47.2 us
  transfers between devices with their start and end apart: 6, of which 6 were waited for; matrix products, arithmetic and copies ran while one was open for 1% of the time, Pallas kernels for 0%

commit v1 on v0

--- a/solution.py
+++ b/solution.py
@@ -99,8 +99,14 @@
         col_root = pivot % front_count
         col_slot = pivot // front_count
         column = from_root(parent[:, col_slot * block : (col_slot + 1) * block], "front", col_root)
-        whole = lax.all_gather(
-            column.reshape(parent_rslots, 1, block, block), "leaf", axis=1, tiled=True
+        whole = jnp.concatenate(
+            lax.all_to_all(
+                jnp.stack([column.reshape(parent_rslots, 1, block, block)] * lax.axis_size("leaf")),
+                "leaf",
+                0,
+                0,
+            ),
+            axis=1,
         )
         whole = whole.reshape(parent_blocks * block, block)
         factor = jnp.linalg.cholesky(whole[pivot * block : (pivot + 1) * block])

time: 1130 us -> 1170 us (1.035)
  starting transfers between devices: 8.29 us -> 27.7 us
  waiting for transfers between devices: 519 us -> 536 us
    all_to_all x0 -> x2, waiting for transfers between devices: none -> 92.6 us  [body(): lax.all_to_all(jnp.stack([column.reshape(parent_rslots, 1, block, block)]...]
    all_gather x2 -> x0, waiting for transfers between devices: 71.3 us -> none  [body(): lax.all_gather(column.reshape(parent_rslots, 1, block, block), 'leaf', ax...]
    all_to_all x0 -> x2, starting transfers between devices: none -> 19.7 us  [body(): lax.all_to_all(jnp.stack([column.reshape(parent_rslots, 1, block, block)]...]
    another operation x0 -> x4, local copies, waits for them, and re-layouts: none -> 15.5 us  [the longest x2 10 us: body(): whole = whole.reshape(parent_blocks * block, block)]
    unnamed x57 -> x51, local copies, waits for them, and re-layouts: 45.1 us -> 30.3 us
    reshape x0 -> x2, local copies, waits for them, and re-layouts: none -> 13.2 us  [body(): jnp.concatenate(lax.all_to_all(jnp.stack([column.reshape(parent_rslots, 1...]
where the time goes in v1:
time: 1170 us; the launch traced here: 1160 us
  waiting for transfers between devices  536 us (46%)
  other arithmetic  281 us (24%)
  matrix products  136 us (12%)
  local copies, waits for them, and re-layouts  106 us (9%)
  blocking collectives  58.8 us (5%)
  starting transfers between devices  27.7 us (2%)
  between operations  15.3 us (1%)
    psum x2, waiting for transfers between devices, from_root(): return lax.psum(kept, axis)  277 us
    all_gather x1, waiting for transfers between devices, body(): panel = lax.all_gather(rows_part, 'front', axis=0, tiled=True)  147 us
    another operation x20, other arithmetic, solve_rows(): return jax.scipy.linalg.solve_triangular(factor, rows.T, lower=True).T  105 us
    another operation x24, other arithmetic, body(): factor = jnp.linalg.cholesky(current[start:finish])  99.7 us
    all_to_all x2, waiting for transfers between devices, body(): lax.all_to_all(jnp.stack([column.reshape(parent_rslots, 1, block, block)]...  92.6 us
    dot_general x7, matrix products, body(): current = current - jnp.dot(done, done[start:finish].T, precision=highest)  59.9 us
    all_to_all x1, blocking collectives, body(): lax.all_to_all(leading, 'front', split_axis=0, concat_axis=3, tiled=True)  58.8 us
    another operation x10, matrix products, solve_rows(): return jax.scipy.linalg.solve_triangular(factor, rows.T, lower=True).T  41.1 us
  transfers between devices with their start and end apart: 6, of which 6 were waited for; matrix products, arithmetic and copies ran while one was open for 1% of the time, Pallas kernels for 0%

profile of v1, /device:TPU:1, one launch (start us, length us, event | category | flops | bytes accessed | tf_op | source)
XLA Modules:
  0.0 1160.5 jit_solution(11489920185497049005)
XLA Ops:
  9.1 58.8 %all_to_all.30 = f32[32,128,1,1,128]{1,4,3,2,0:T(8,128)S(1)} all-to-all(f32[32,128,1,1,128]{1,4,3,2,0:T(8,128)S(1)} %copy.146), channel_id=1, replica_groups=mesh['leaf'=8,'front'=32] {'front'}, dimensions={0} | all-to-all | bytes 4194304 | tf_op jit(solution)/shard_map/all_to_all | solution.py:37
  70.8 147.3 %all-gather.2.cloned.1.call-done = f32[4096,1024]{0,1:T(8,128)} async-done(((f32[128,1024]{0,1:T(8,128)}), f32[4096,1024]{0,1:T(8,128)}) %all-gather.2.cloned.1.call-update) | async-done | bytes 16777232 | tf_op jit(solution)/shard_map/all_gather | solution.py:39
  219.9 11.7 %cholesky.164 = f32[128,128]{1,0:T(8,128)S(1)} custom-call(f32[128,128]{1,0:T(8,128)S(1)} %fusion.173), custom_call_target="Cholesky" | custom-call | tf_op jit(solution)/shard_map/jit(cholesky)/cholesky | solution.py:48
  256.6 11.9 %cholesky.175 = f32[128,128]{1,0:T(8,128)S(1)} custom-call(f32[128,128]{1,0:T(8,128)S(1)} %fusion.171), custom_call_target="Cholesky" | custom-call | tf_op jit(solution)/shard_map/jit(cholesky)/cholesky | solution.py:48
  291.5 12.1 %cholesky.186 = f32[128,128]{1,0:T(8,128)S(1)} custom-call(f32[128,128]{1,0:T(8,128)S(1)} %fusion.169), custom_call_target="Cholesky" | custom-call | tf_op jit(solution)/shard_map/jit(cholesky)/cholesky | solution.py:48
  329.4 11.7 %cholesky.197 = f32[128,128]{1,0:T(8,128)S(1)} custom-call(f32[128,128]{1,0:T(8,128)S(1)} %fusion.167), custom_call_target="Cholesky" | custom-call | tf_op jit(solution)/shard_map/jit(cholesky)/cholesky | solution.py:48
  357.0 10.2 fusion.41
  369.6 11.7 %cholesky.208 = f32[128,128]{1,0:T(8,128)S(1)} custom-call(f32[128,128]{1,0:T(8,128)S(1)} %fusion.165), custom_call_target="Cholesky" | custom-call | tf_op jit(solution)/shard_map/jit(cholesky)/cholesky | solution.py:48
  414.2 10.0 convolution_subtract_fusion.1
  424.3 11.7 %cholesky.219 = f32[128,128]{1,0:T(8,128)S(1)} custom-call(f32[128,128]{1,0:T(8,128)S(1)} %fusion.163), custom_call_target="Cholesky" | custom-call | tf_op jit(solution)/shard_map/jit(cholesky)/cholesky | solution.py:48
  454.9 10.7 convolution_subtract_fusion
  465.7 11.7 %cholesky.230 = f32[128,128]{1,0:T(8,128)S(1)} custom-call(f32[128,128]{1,0:T(8,128)S(1)} %fusion.161), custom_call_target="Cholesky" | custom-call | tf_op jit(solution)/shard_map/jit(cholesky)/cholesky | solution.py:48
  495.4 12.9 %convolution_subtract_fusion.4 = f32[4096,128]{0,1:T(8,128)S(1)} fusion(f32[4096,896]{0,1:T(8,128)} %get-tuple-element.91, f32[4096,1024]{0,1:T(8,128)} %all-gather.2.cloned.1.call-done), kind=kOutput, calls=%fused_computation.48 | convolution fusion | flops 5637668864 | bytes 19333120 | tf_op jit(solution)/shard_map/dot_general | solution.py:47
  508.4 11.7 %cholesky.241 = f32[128,128]{1,0:T(8,128)S(1)} custom-call(f32[128,128]{1,0:T(8,128)S(1)} %fusion.159), custom_call_target="Cholesky" | custom-call | tf_op jit(solution)/shard_map/jit(cholesky)/cholesky | solution.py:48
  537.0 10.8 slice.282
  566.9 21.1 %convolution_subtract_fusion.5 = f32[3072,128]{1,0:T(8,128)} fusion(f32[128,1024]{0,1:T(8,128)S(1)} %bitcast.234, f32[1,4096,1,1,128]{4,1,3,2,0:T(8,128)S(1)} %bitcast.221, f32[4096,1024]{0,1:T(8,128)S(1)} %bitcast.211), kind=kOutput, calls=%fused_computation.64 | convolution fusion | flops 4832231424 | bytes 16252928 | tf_op jit(solution)/shard_map/dot_general | solution.py:56
  604.2 19.8 %all-to-all-done.1 = f32[3,8,128,1,128]{4,2,0,3,1:T(8,128)} async-done(((f32[3,8,128,1,128]{4,2,0,3,1:T(8,128)}), f32[3,8,128,1,128]{4,2,0,3,1:T(8,128)}, u32[]{:S(2)}, u32[]{:S(2)}) %all-to-all-start.1) | async-done | bytes 1572896 | tf_op jit(solution)/shard_map/all_to_all | solution.py:75
  635.1 138.2 %all-reduce.4.cloned.1.call-done = f32[8,128,128]{2,1,0:T(8,128)} async-done(((f32[8,128,128]{2,1,0:T(8,128)}), f32[8,128,128]{2,1,0:T(8,128)}) %all-reduce.4.cloned.1.call-update) | async-done | bytes 524304 | tf_op jit(solution)/shard_map/psum | solution.py:12
  786.5 48.8 %all-to-all-done.2 = f32[8,8,1,128,128]{3,1,4,2,0:T(8,128)} async-done(((f32[8,8,1,128,128]{3,1,4,2,0:T(8,128)}), f32[8,8,1,128,128]{3,1,4,2,0:T(8,128)}, u32[]{:S(2)}, u32[]{:S(2)}) %all-to-all-start.2) | async-done | bytes 4194336 | tf_op jit(solution)/shard_map/all_to_all | solution.py:103
  848.9 11.7 %cholesky.252 = f32[128,128]{1,0:T(8,128)S(1)} custom-call(f32[128,128]{1,0:T(8,128)S(1)} %fusion.157), custom_call_target="Cholesky" | custom-call | tf_op jit(solution)/shard_map/jit(cholesky)/cholesky | solution.py:112
  892.5 138.3 %all-reduce.6.cloned.1.call-done = f32[8,128,128]{2,1,0:T(8,128)} async-done(((f32[8,128,128]{2,1,0:T(8,128)}), f32[8,128,128]{2,1,0:T(8,128)}) %all-reduce.6.cloned.1.call-update) | async-done | bytes 524304 | tf_op jit(solution)/shard_map/psum | solution.py:12
  1036.1 10.1 all-to-all-start.3
  1051.3 43.7 %all-to-all-done.3 = f32[8,8,1,128,128]{3,1,4,2,0:T(8,128)} async-done(((f32[8,8,1,128,128]{3,1,4,2,0:T(8,128)}), f32[8,8,1,128,128]{3,1,4,2,0:T(8,128)}, u32[]{:S(2)}, u32[]{:S(2)}) %all-to-all-start.3) | async-done | bytes 4194336 | tf_op jit(solution)/shard_map/all_to_all | solution.py:103
  1108.4 11.7 %cholesky.263 = f32[128,128]{1,0:T(8,128)S(1)} custom-call(f32[128,128]{1,0:T(8,128)S(1)} %fusion.155), custom_call_target="Cholesky" | custom-call | tf_op jit(solution)/shard_map/jit(cholesky)/cholesky | solution.py:112
  (226 shorter events, 346.8 us)
Async XLA Ops:
  7.2 211.0 %all-gather.2.cloned.1.call-start = ((), (), s32[]{:S(2)}) async-start(), calls=%async_computation.4 | async-start | bytes 17301504 | tf_op jit(solution)/shard_map/all_gather | solution.py:39
  68.9 177.4 %copy-start.15 = (pred[4096]{0:T(1024)(128)(4,1)}, pred[4096]{0:T(1024)(128)(4,1)S(1)}, u32[]{:S(2)}) copy-start(pred[4096]{0:T(1024)(128)(4,1)S(1)} %fusion.195) | copy-start | bytes 12292
  368.6 28.3 %copy-start.2 = (f32[3840,128]{0,1:T(8,128)S(1)}, f32[3840,128]{0,1:T(8,128)}, u32[]{:S(2)}) copy-start(f32[3840,128]{0,1:T(8,128)} %fusion.62) | copy-start | bytes 5898244
  396.9 4.4 copy-start.7
  401.3 4.3 copy-start.8
  405.6 4.2 copy-start.9
  547.8 19.0 %slice-start = ((s8[16777216]{0:T(1024)(128)(4,1)}), s8[4194304]{0:T(1024)(128)(4,1)S(1)}, s32[]{:S(2)}) async-start(s8[16777216]{0:T(1024)(128)(4,1)} %bitcast.210), calls=%async_computation.7 | async-start | bytes 8388608
  547.8 19.0 %slice-start.1 = ((s8[16777216]{0:T(1024)(128)(4,1)}), s8[4194304]{0:T(1024)(128)(4,1)S(1)}, s32[]{:S(2)}) async-start(s8[16777216]{0:T(1024)(128)(4,1)} %bitcast.210), calls=%async_computation.8 | async-start | bytes 8388608
  555.2 11.6 %slice-start.2 = ((s8[16777216]{0:T(1024)(128)(4,1)}), s8[4194304]{0:T(1024)(128)(4,1)S(1)}, s32[]{:S(2)}) async-start(s8[16777216]{0:T(1024)(128)(4,1)} %bitcast.210), calls=%async_computation.9 | async-start | bytes 8388608
  555.2 11.6 %slice-start.3 = ((s8[16777216]{0:T(1024)(128)(4,1)}), s8[4194304]{0:T(1024)(128)(4,1)S(1)}, s32[]{:S(2)}) async-start(s8[16777216]{0:T(1024)(128)(4,1)} %bitcast.210), calls=%async_computation.10 | async-start | bytes 8388608
  555.2 11.6 %copy-start.4 = (f32[1,4096,1,1,128]{4,3,2,1,0:T(1,128)S(1)}, f32[1,4096,1,1,128]{4,3,2,1,0:T(1,128)}, u32[]{:S(2)}) copy-start(f32[1,4096,1,1,128]{4,3,2,1,0:T(1,128)} %param.8) | copy-start | bytes 6291460
  591.4 1.4 copy-start.3
  591.4 1.4 slice-start.4
  595.6 8.0 copy-start.17
  595.6 28.4 %all-to-all-start.1 = ((f32[3,8,128,1,128]{4,2,0,3,1:T(8,128)}), f32[3,8,128,1,128]{4,2,0,3,1:T(8,128)}, u32[]{:S(2)}, u32[]{:S(2)}) async-start(f32[3,8,128,1,128]{4,2,0,3,1:T(8,128)} %copy.183), calls=%async_computation.1 | async-start | bytes 3145728 | tf_op jit(solution)/shard_map/all_to_all | solution.py:75
  603.2 170.1 %all-reduce.4.cloned.1.call-start = ((), (), s32[]{:S(2)}) async-start(), calls=%async_computation.5 | async-start | bytes 1048576 | tf_op jit(solution)/shard_map/psum | solution.py:12
  628.8 4.3 copy-start.14
  776.8 58.6 %all-to-all-start.2 = ((f32[8,8,1,128,128]{3,1,4,2,0:T(8,128)}), f32[8,8,1,128,128]{3,1,4,2,0:T(8,128)}, u32[]{:S(2)}, u32[]{:S(2)}) async-start(f32[8,8,1,128,128]{3,1,4,2,0:T(8,128)} %stack.6), calls=%async_computation.2 | async-start | bytes 8388608 | tf_op jit(solution)/shard_map/all_to_all | solution.py:103
  786.5 244.4 %all-reduce.6.cloned.1.call-start = ((), (), s32[]{:S(2)}) async-start(), calls=%async_computation.6 | async-start | bytes 1048576 | tf_op jit(solution)/shard_map/psum | solution.py:12
  877.2 1.9 copy-start.1
  880.0 8.6 copy-start.11
  1036.1 10.1 copy-start.16
  1036.1 58.9 %all-to-all-start.3 = ((f32[8,8,1,128,128]{3,1,4,2,0:T(8,128)}), f32[8,8,1,128,128]{3,1,4,2,0:T(8,128)}, u32[]{:S(2)}, u32[]{:S(2)}) async-start(f32[8,8,1,128,128]{3,1,4,2,0:T(8,128)} %stack.7), calls=%async_computation.3 | async-start | bytes 8388608 | tf_op jit(solution)/shard_map/all_to_all | solution.py:103
  1137.0 1.9 copy-start
  (5 other events, 6.3 us)
Sparse Core Ops, SparseCore 0:
  68.9 149.1 all-gather.1
  635.2 138.0 all-reduce.3
  892.6 138.1 all-reduce.5
